TPU v7x, 128 devices: a whole 4x4x4 slice. The times are simulated.
128 devices in a mesh: row: 8 (over y_hi, x), col: 16 (over y_lo, z, core).
Axes of the slice: x: 4, y: 4 (y_hi: 2, y_lo: 2; y = y_hi * 2 + y_lo), z: 4, core: 2. Of those that a mesh axis runs over, the one named last changes fastest.
Arguments:
- right_side: float32 [16, 512, 512], P('col', 'row'), may hold values from -6 to 6
- affinity_blocks: float32 [16, 16, 8, 128, 128], P('row', 'col'), may hold values from -0.03125 to 0.03125
- block_coords: int32 [16, 16, 8, 2], P('row', 'col'), may hold values from 0 to 3
- block_counts: int32 [16, 16], P('row', 'col'), may hold values from 4 to 8, as said below
Outputs:
- ranking: float32 [16, 512, 512], P('col', 'row')
- residual: float32 [16, 512, 512], P('col', 'row')
Inputs may be any that keep to these rules, and one draw needn't show every extreme that they name: `block_counts`: some grid tile holds 8 live blocks in every draw.
All inputs are finite; a program needn't handle non-finite values.
Results may differ from a plain program's by a relative error of at most 0.0003.
Values sent between devices are 32-bit elements; how exact they have to be, the bound alone decides.
No kernel may reach another device: no remote copies, remote signals or barrier semaphores. Data moves between devices by JAX's collectives and lax.ppermute only.
A program may use at most 64 MiB of HBM per device.

v0:
```python
import jax
import jax.numpy as jnp
from jax import lax
from jax.sharding import PartitionSpec as P

ITERS = 3
diffusion = 0.8


def broadcast(value, axis, source):
    kept = jnp.where(lax.axis_index(axis) == source, value, 0).astype(value.dtype)
    return lax.psum(kept, axis)


def live_blocks(blocks, count):
    live = (jnp.arange(blocks.shape[0], dtype=jnp.int32) < count).astype(blocks.dtype)
    return blocks * live[:, None, None]


def forward_only(masked, rows, cols, column_field):
    position = jnp.arange(column_field.shape[0], dtype=jnp.int32)
    picked = jnp.take(column_field, cols, axis=0)
    product = jnp.einsum("kab,kbw->kaw", masked, picked, precision=lax.Precision.HIGHEST)
    row_onehot = (rows[None, :] == position[:, None]).astype(jnp.float32)
    return jnp.einsum("tk,kaw->taw", row_onehot, product, precision=lax.Precision.HIGHEST)


def backward_only(masked, rows, cols, row_field):
    position = jnp.arange(row_field.shape[0], dtype=jnp.int32)
    chosen = jnp.take(row_field, rows, axis=0)
    mirrored = jnp.einsum("kab,kaw->kbw", masked, chosen, precision=lax.Precision.HIGHEST)
    col_onehot = (cols[None, :] == position[:, None]).astype(jnp.float32)
    return jnp.einsum("tk,kbw->tbw", col_onehot, mirrored, precision=lax.Precision.HIGHEST)


def tile_products(masked, rows, cols, column_field, row_field):
    forward = forward_only(masked, rows, cols, column_field)
    backward = backward_only(masked, rows, cols, row_field)
    return (forward, backward)


def block_products(affinity_blocks, block_coords, block_counts, column_block, row_blocks):
    members = affinity_blocks.shape[0]
    edge = affinity_blocks.shape[-1]
    width = column_block.shape[1]
    column_field = column_block.reshape(-1, edge, width)
    forward_parts = []
    backward_total = jnp.zeros(column_field.shape, jnp.float32)
    for member in range(members):
        masked = live_blocks(affinity_blocks[member, 0], block_counts[member, 0])
        forward, backward = tile_products(
            masked,
            block_coords[member, 0, :, 0],
            block_coords[member, 0, :, 1],
            column_field,
            row_blocks[member].reshape(column_field.shape),
        )
        forward_parts.append(forward.reshape(column_block.shape))
        backward_total = backward_total + backward
    return (jnp.stack(forward_parts), backward_total.reshape(column_block.shape))


def operate(piece, affinity_blocks, block_coords, block_counts):
    rows_count = lax.axis_size("row")
    cols_count = lax.axis_size("col")
    members = cols_count // rows_count
    my_row = lax.axis_index("row")
    share = piece.shape[1]
    width = piece.shape[2]
    sliver = share // cols_count
    whole = lax.all_gather(piece, "row", axis=1, tiled=True)
    received = []
    for member in range(members):
        received.append(broadcast(whole[0], "col", my_row * members + member))
    row_blocks = jnp.stack(received)
    forward, backward = block_products(
        affinity_blocks, block_coords, block_counts, whole[0], row_blocks
    )
    back_part = lax.psum_scatter(backward[None], "row", scatter_dimension=1, tiled=True)
    spread = forward.reshape(members, rows_count, cols_count, sliver, width)
    summed = lax.psum_scatter(spread, "col", scatter_dimension=2, tiled=True)
    ordered = summed.reshape(members, rows_count, sliver, width).transpose(1, 0, 2, 3)
    ordered = ordered.reshape(rows_count * members, sliver, width)
    forward_part = lax.all_to_all(
        lax.all_to_all(ordered, "row", split_axis=0, concat_axis=0, tiled=True),
        "col",
        split_axis=0,
        concat_axis=1,
        tiled=True,
    )
    return piece - diffusion * (forward_part + back_part)


def squares(residual):
    return lax.psum(jnp.sum(residual * residual, axis=(0, 1)), ("row", "col"))


def shards(right_side, affinity_blocks, block_coords, block_counts):
    ranking = jnp.zeros_like(right_side)
    residual = right_side
    direction = right_side
    norm_now = squares(residual)
    for step in range(ITERS):
        image = operate(direction, affinity_blocks, block_coords, block_counts)
        curve = lax.psum(jnp.sum(direction * image, axis=(0, 1)), ("row", "col"))
        alpha = norm_now / curve
        ranking = ranking + alpha * direction
        residual = residual - alpha * image
        if step + 1 < ITERS:
            norm_next = squares(residual)
            direction = residual + norm_next / norm_now * direction
            norm_now = norm_next
    return (ranking, residual)


def solution(mesh):
    in_specs = (
        P("col", "row", None),
        P("row", "col", None, None, None),
        P("row", "col", None, None),
        P("row", "col"),
    )
    out_specs = (P("col", "row", None), P("col", "row", None))
    return jax.shard_map(shards, mesh=mesh, in_specs=in_specs, out_specs=out_specs, check_vma=False)
```

profile of v0, /device:TPU:1, one launch (start us, length us, event | category | flops | bytes accessed | tf_op | source)
XLA Modules:
  0.0 1282.6 jit_solution(11291299337467463532)
XLA Ops:
  9.9 50.0 %all-gather.4.cloned.1.call-done = f32[1,512,512]{2,1,0:T(8,128)} async-done(((f32[1,64,512]{2,1,0:T(8,128)}), f32[1,512,512]{2,1,0:T(8,128)}) %all-gather.4.cloned.1.call-update) | async-done | bytes 1048592 | tf_op jit(solution)/shard_map/all_gather | solution.py:71
  60.0 2.9 broadcast_select_fusion.5
  63.8 2.1 gather_fusion.1
  65.9 3.6 fusion.44
  69.5 2.2 fusion.20
  75.3 3.6 fusion.46
  79.0 2.2 fusion.22
  84.6 2.6 copy.49
  87.5 98.5 %all-reduce.12.cloned.1.call-done = (f32[4,128,512]{2,1,0:T(8,128)}, f32[4,128,512]{2,1,0:T(8,128)}) async-done(((f32[4,128,512]{2,1,0:T(8,128)}, f32[4,128,512]{2,1,0:T(8,128)}), (f32[4,128,512]{2,1,0:T(8,128)}, f32[4,128,512]{2,1,0:T(8,128)})) %all-reduce.12.cloned.1.call-update) | async-done | bytes 2097168 | tf_op jit(solution)/shard_map/psum | solution.py:12
  186.0 3.2 gather_fusion.3
  191.2 3.7 fusion.40
  194.9 2.2 fusion.16
  197.1 2.2 fusion.42
  199.3 2.3 fusion.48
  203.0 46.3 %reduce-scatter.7.cloned.1.call-done = f32[2,8,1,4,512]{4,1,3,0,2:T(8,128)} async-done(((f32[2,8,16,4,512]{4,1,3,0,2:T(8,128)}), f32[2,8,1,4,512]{4,1,3,0,2:T(8,128)}) %reduce-scatter.7.cloned.1.call-update) | async-done | bytes 131088 | tf_op jit(solution)/shard_map/reduce_scatter | solution.py:81
  250.3 13.3 %all_to_all.51 = f32[16,4,512]{2,1,0:T(4,128)S(1)} all-to-all(f32[16,4,512]{2,1,0:T(4,128)S(1)} %bitcast.97), channel_id=1, replica_groups=mesh['row'=8,'col'=16] {'row'}, dimensions={0} | all-to-all | bytes 262144 | tf_op jit(solution)/shard_map/all_to_all | solution.py:85
  263.6 14.2 %all_to_all.52 = f32[16,4,512]{2,1,0:T(4,128)S(1)} all-to-all(f32[16,4,512]{2,1,0:T(4,128)S(1)} %all_to_all.51), channel_id=1, replica_groups=mesh['row'=8,'col'=16] {'col'}, dimensions={0} | all-to-all | bytes 262144 | tf_op jit(solution)/shard_map/all_to_all | solution.py:84
  277.8 47.4 %reduce-scatter.9.cloned.1.call-done = f32[1,64,512]{2,1,0:T(8,128)} async-done(((f32[1,512,512]{2,1,0:T(8,128)}), f32[1,64,512]{2,1,0:T(8,128)}) %reduce-scatter.9.cloned.1.call-update) | async-done | bytes 131088 | tf_op jit(solution)/shard_map/reduce_scatter | solution.py:79
  326.1 66.3 %all-reduce = (f32[512]{0:T(512)S(1)}, f32[512]{0:T(512)S(1)}) all-reduce(f32[512]{0:T(512)S(1)} %get-tuple-element.4, f32[512]{0:T(512)S(1)} %get-tuple-element.3), channel_id=1, replica_groups=mesh['row'=8,'col'=16] {'row','col'}, use_global_device_ids=true, to_apply=%region_1.0 | all-reduce | flops 1024 | bytes 8192 | tf_op jit(solution)/shard_map/psum | solution.py:95
  393.4 62.5 %psum.88 = f32[512]{0:T(512)S(1)} all-reduce(f32[512]{0:T(512)S(1)} %get-tuple-element.15), channel_id=1, replica_groups=mesh['row'=8,'col'=16] {'row','col'}, use_global_device_ids=true, to_apply=%region_9.11 | all-reduce | flops 512 | bytes 4096 | tf_op jit(solution)/shard_map/psum | solution.py:95
  456.7 43.6 %all-gather.6.cloned.1.call-done = f32[1,512,512]{2,1,0:T(8,128)} async-done(((f32[1,64,512]{2,1,0:T(8,128)}), f32[1,512,512]{2,1,0:T(8,128)}) %all-gather.6.cloned.1.call-update) | async-done | bytes 1048592 | tf_op jit(solution)/shard_map/all_gather | solution.py:71
  500.3 2.9 broadcast_select_fusion.3
  503.8 2.1 gather_fusion.5
  505.8 2.1 gather_fusion.4
  507.9 3.6 fusion.36
  511.5 2.2 fusion.12
  515.1 2.5 stack.25
  517.6 2.0 fusion.38
  519.7 2.2 fusion.14
  525.3 2.6 copy.60
  528.2 98.3 %all-reduce.10.cloned.1.call-done = (f32[4,128,512]{2,1,0:T(8,128)}, f32[4,128,512]{2,1,0:T(8,128)}) async-done(((f32[4,128,512]{2,1,0:T(8,128)}, f32[4,128,512]{2,1,0:T(8,128)}), (f32[4,128,512]{2,1,0:T(8,128)}, f32[4,128,512]{2,1,0:T(8,128)})) %all-reduce.10.cloned.1.call-update) | async-done | bytes 2097168 | tf_op jit(solution)/shard_map/psum | solution.py:12
  626.4 3.2 gather_fusion.7
  631.6 3.7 fusion.32
  635.3 2.2 fusion.8
  637.5 2.2 fusion.34
  639.7 2.3 fusion.51
  643.4 46.4 %reduce-scatter.11.cloned.1.call-done = f32[2,8,1,4,512]{4,1,3,0,2:T(8,128)} async-done(((f32[2,8,16,4,512]{4,1,3,0,2:T(8,128)}), f32[2,8,1,4,512]{4,1,3,0,2:T(8,128)}) %reduce-scatter.11.cloned.1.call-update) | async-done | bytes 131088 | tf_op jit(solution)/shard_map/reduce_scatter | solution.py:81
  690.8 13.3 %all_to_all.53 = f32[16,4,512]{2,1,0:T(4,128)S(1)} all-to-all(f32[16,4,512]{2,1,0:T(4,128)S(1)} %bitcast.98), channel_id=1, replica_groups=mesh['row'=8,'col'=16] {'row'}, dimensions={0} | all-to-all | bytes 262144 | tf_op jit(solution)/shard_map/all_to_all | solution.py:85
  704.1 14.3 %all_to_all.54 = f32[16,4,512]{2,1,0:T(4,128)S(1)} all-to-all(f32[16,4,512]{2,1,0:T(4,128)S(1)} %all_to_all.53), channel_id=1, replica_groups=mesh['row'=8,'col'=16] {'col'}, dimensions={0} | all-to-all | bytes 262144 | tf_op jit(solution)/shard_map/all_to_all | solution.py:84
  718.4 47.8 %reduce-scatter.13.cloned.1.call-done = f32[1,64,512]{2,1,0:T(8,128)} async-done(((f32[1,512,512]{2,1,0:T(8,128)}), f32[1,64,512]{2,1,0:T(8,128)}) %reduce-scatter.13.cloned.1.call-update) | async-done | bytes 131088 | tf_op jit(solution)/shard_map/reduce_scatter | solution.py:79
  767.2 66.3 %psum.91 = f32[512]{0:T(512)S(1)} all-reduce(f32[512]{0:T(512)S(1)} %multiply_reduce_fusion.2), channel_id=1, replica_groups=mesh['row'=8,'col'=16] {'row','col'}, use_global_device_ids=true, to_apply=%region_15.17 | all-reduce | flops 512 | bytes 4096 | tf_op jit(solution)/shard_map/psum | solution.py:105
  834.5 62.5 %psum.92 = f32[512]{0:T(512)S(1)} all-reduce(f32[512]{0:T(512)S(1)} %get-tuple-element.13), channel_id=1, replica_groups=mesh['row'=8,'col'=16] {'row','col'}, use_global_device_ids=true, to_apply=%region_17.19 | all-reduce | flops 512 | bytes 4096 | tf_op jit(solution)/shard_map/psum | solution.py:95
  897.8 43.6 %all-gather.8.cloned.1.call-done = f32[1,512,512]{2,1,0:T(8,128)} async-done(((f32[1,64,512]{2,1,0:T(8,128)}), f32[1,512,512]{2,1,0:T(8,128)}) %all-gather.8.cloned.1.call-update) | async-done | bytes 1048592 | tf_op jit(solution)/shard_map/all_gather | solution.py:71
  941.4 3.0 broadcast_select_fusion.1
  944.8 2.2 gather_fusion.9
  947.0 2.3 gather_fusion.8
  949.4 3.6 fusion.28
  953.0 2.2 fusion.4
  956.6 2.5 stack.28
  959.1 2.0 fusion.30
  961.1 2.2 fusion.6
  966.8 2.6 copy.71
  969.6 97.9 %all-reduce.8.cloned.1.call-done = (f32[4,128,512]{2,1,0:T(8,128)}, f32[4,128,512]{2,1,0:T(8,128)}) async-done(((f32[4,128,512]{2,1,0:T(8,128)}, f32[4,128,512]{2,1,0:T(8,128)}), (f32[4,128,512]{2,1,0:T(8,128)}, f32[4,128,512]{2,1,0:T(8,128)})) %all-reduce.8.cloned.1.call-update) | async-done | bytes 2097168 | tf_op jit(solution)/shard_map/psum | solution.py:12
  1067.5 3.4 gather_fusion.11
  1070.8 2.0 gather_fusion.10
  1072.9 3.7 fusion.24
  1076.6 2.2 fusion
  1078.9 2.2 fusion.26
  1081.0 2.3 fusion.54
  1084.7 46.0 %reduce-scatter.15.cloned.1.call-done = f32[2,8,1,4,512]{4,1,3,0,2:T(8,128)} async-done(((f32[2,8,16,4,512]{4,1,3,0,2:T(8,128)}), f32[2,8,1,4,512]{4,1,3,0,2:T(8,128)}) %reduce-scatter.15.cloned.1.call-update) | async-done | bytes 131088 | tf_op jit(solution)/shard_map/reduce_scatter | solution.py:81
  1131.8 13.3 %all_to_all.55 = f32[16,4,512]{2,1,0:T(4,128)S(1)} all-to-all(f32[16,4,512]{2,1,0:T(4,128)S(1)} %bitcast.99), channel_id=1, replica_groups=mesh['row'=8,'col'=16] {'row'}, dimensions={0} | all-to-all | bytes 262144 | tf_op jit(solution)/shard_map/all_to_all | solution.py:85
  1145.0 14.2 %all_to_all.56 = f32[16,4,512]{2,1,0:T(4,128)S(1)} all-to-all(f32[16,4,512]{2,1,0:T(4,128)S(1)} %all_to_all.55), channel_id=1, replica_groups=mesh['row'=8,'col'=16] {'col'}, dimensions={0} | all-to-all | bytes 262144 | tf_op jit(solution)/shard_map/all_to_all | solution.py:84
  1159.3 47.4 %reduce-scatter.17.cloned.1.call-done = f32[1,64,512]{2,1,0:T(8,128)} async-done(((f32[1,512,512]{2,1,0:T(8,128)}), f32[1,64,512]{2,1,0:T(8,128)}) %reduce-scatter.17.cloned.1.call-update) | async-done | bytes 131088 | tf_op jit(solution)/shard_map/reduce_scatter | solution.py:79
  1207.6 66.3 %psum.95 = f32[512]{0:T(512)S(1)} all-reduce(f32[512]{0:T(512)S(1)} %multiply_reduce_fusion), channel_id=1, replica_groups=mesh['row'=8,'col'=16] {'row','col'}, use_global_device_ids=true, to_apply=%region_23.25 | all-reduce | flops 512 | bytes 4096 | tf_op jit(solution)/shard_map/psum | solution.py:105
  (143 shorter events, 40.8 us)
Async XLA Ops:
  7.2 52.8 %all-gather.4.cloned.1.call-start = ((), (), s32[]{:S(2)}) async-start(), calls=%async_computation.12 | async-start | bytes 1179648 | tf_op jit(solution)/shard_map/all_gather | solution.py:71
  7.9 178.1 %all-reduce.12.cloned.1.call-start = ((), (), s32[]{:S(2)}) async-start(), calls=%async_computation.23 | async-start | bytes 4194304 | tf_op jit(solution)/shard_map/psum | solution.py:12
  9.9 53.7 %copy-start.26 = (s32[2,1,8,2]{2,3,1,0:T(2,128)S(1)}, s32[2,1,8,2]{2,3,1,0:T(2,128)}, u32[]{:S(2)}) copy-start(s32[2,1,8,2]{2,3,1,0:T(2,128)} %param.8) | copy-start | bytes 388
  60.0 3.8 copy-start.1
  62.9 186.4 %reduce-scatter.7.cloned.1.call-start = ((), (), s32[]{:S(2)}) async-start(), calls=%async_computation.13 | async-start | bytes 2228224 | tf_op jit(solution)/shard_map/reduce_scatter | solution.py:81
  63.7 444.2 %copy-start.22 = (pred[8]{0:T(512)(128)(4,1)}, pred[8]{0:T(512)(128)(4,1)S(1)}, u32[]{:S(2)}) copy-start(pred[8]{0:T(512)(128)(4,1)S(1)} %get-tuple-element.37) | copy-start | bytes 28
  63.7 454.0 %copy-start.20 = (pred[8]{0:T(512)(128)(4,1)}, pred[8]{0:T(512)(128)(4,1)S(1)}, u32[]{:S(2)}) copy-start(pred[8]{0:T(512)(128)(4,1)S(1)} %get-tuple-element.41) | copy-start | bytes 28
  63.7 567.9 %copy-start.18 = (pred[8]{0:T(512)(128)(4,1)}, pred[8]{0:T(512)(128)(4,1)S(1)}, u32[]{:S(2)}) copy-start(pred[8]{0:T(512)(128)(4,1)S(1)} %get-tuple-element.39) | copy-start | bytes 28
  63.7 573.8 %copy-start.16 = (pred[8]{0:T(512)(128)(4,1)}, pred[8]{0:T(512)(128)(4,1)S(1)}, u32[]{:S(2)}) copy-start(pred[8]{0:T(512)(128)(4,1)S(1)} %get-tuple-element.17) | copy-start | bytes 28
  63.7 440.0 %copy-start.36 = (s32[1024]{0:T(1024)}, s32[1024]{0:T(1024)S(1)}, u32[]{:S(2)}) copy-start(s32[1024]{0:T(1024)S(1)} %get-tuple-element.47) | copy-start | bytes 12292
  63.7 442.1 %copy-start.35 = (s32[1024]{0:T(1024)}, s32[1024]{0:T(1024)S(1)}, u32[]{:S(2)}) copy-start(s32[1024]{0:T(1024)S(1)} %get-tuple-element.48) | copy-start | bytes 12292
  63.8 447.8 %copy-start.31 = (s32[8]{0:T(128)}, s32[8]{0:T(128)S(1)}, u32[]{:S(2)}) copy-start(s32[8]{0:T(128)S(1)} %get-tuple-element.36) | copy-start | bytes 100
  63.8 455.9 %copy-start.29 = (s32[8]{0:T(128)}, s32[8]{0:T(128)S(1)}, u32[]{:S(2)}) copy-start(s32[8]{0:T(128)S(1)} %get-tuple-element.34) | copy-start | bytes 100
  63.8 571.5 %copy-start.27 = (s32[8]{0:T(128)}, s32[8]{0:T(128)S(1)}, u32[]{:S(2)}) copy-start(s32[8]{0:T(128)S(1)} %get-tuple-element.35) | copy-start | bytes 100
  63.8 575.9 %copy-start.24 = (s32[8]{0:T(128)}, s32[8]{0:T(128)S(1)}, u32[]{:S(2)}) copy-start(s32[8]{0:T(128)S(1)} %get-tuple-element.33) | copy-start | bytes 100
  63.8 2.1 copy-start
  81.2 1.7 copy-start.7
  87.2 238.0 %reduce-scatter.9.cloned.1.call-start = ((), (), s32[]{:S(2)}) async-start(), calls=%async_computation.14 | async-start | bytes 1179648 | tf_op jit(solution)/shard_map/reduce_scatter | solution.py:79
  87.5 539.0 %copy-start.34 = (s32[1024]{0:T(1024)}, s32[1024]{0:T(1024)S(1)}, u32[]{:S(2)}) copy-start(s32[1024]{0:T(1024)S(1)} %get-tuple-element.45) | copy-start | bytes 12292
  87.5 542.2 %copy-start.33 = (s32[1024]{0:T(1024)}, s32[1024]{0:T(1024)S(1)}, u32[]{:S(2)}) copy-start(s32[1024]{0:T(1024)S(1)} %get-tuple-element.46) | copy-start | bytes 12292
  201.6 123.6 %copy-start.10 = (f32[1,64,512]{2,1,0:T(8,128)S(1)}, f32[1,64,512]{2,1,0:T(8,128)}, u32[]{:S(2)}) copy-start(f32[1,64,512]{2,1,0:T(8,128)} %param.6) | copy-start | bytes 393220
  202.9 297.4 %all-gather.6.cloned.1.call-start = ((), (), s32[]{:S(2)}) async-start(), calls=%async_computation.15 | async-start | bytes 1179648 | tf_op jit(solution)/shard_map/all_gather | solution.py:71
  456.7 169.7 %all-reduce.10.cloned.1.call-start = ((), (), s32[]{:S(2)}) async-start(), calls=%async_computation.22 | async-start | bytes 4194304 | tf_op jit(solution)/shard_map/psum | solution.py:12
  500.3 3.4 copy-start.3
  503.3 186.5 %reduce-scatter.11.cloned.1.call-start = ((), (), s32[]{:S(2)}) async-start(), calls=%async_computation.16 | async-start | bytes 2228224 | tf_op jit(solution)/shard_map/reduce_scatter | solution.py:81
  513.7 3.9 copy-start.5
  521.9 1.7 copy-start.9
  527.9 238.3 %reduce-scatter.13.cloned.1.call-start = ((), (), s32[]{:S(2)}) async-start(), calls=%async_computation.17 | async-start | bytes 1179648 | tf_op jit(solution)/shard_map/reduce_scatter | solution.py:79
  642.0 124.2 %copy-start.6 = (f32[1,64,512]{2,1,0:T(8,128)S(1)}, f32[1,64,512]{2,1,0:T(8,128)}, u32[]{:S(2)}) copy-start(f32[1,64,512]{2,1,0:T(8,128)} %multiply_add_fusion.2) | copy-start | bytes 393220
  643.4 298.0 %all-gather.8.cloned.1.call-start = ((), (), s32[]{:S(2)}) async-start(), calls=%async_computation.18 | async-start | bytes 1179648 | tf_op jit(solution)/shard_map/all_gather | solution.py:71
  833.5 64.3 %copy-start.14 = (f32[512]{0:T(512)}, f32[512]{0:T(512)S(1)}, u32[]{:S(2)}) copy-start(f32[512]{0:T(512)S(1)} %div.17) | copy-start | bytes 6148
  834.5 63.3 %copy-start.12 = (f32[1,64,512]{2,1,0:T(8,128)}, f32[1,64,512]{2,1,0:T(8,128)S(1)}, u32[]{:S(2)}) copy-start(f32[1,64,512]{2,1,0:T(8,128)S(1)} %get-tuple-element.14) | copy-start | bytes 393220
  897.8 169.7 %all-reduce.8.cloned.1.call-start = ((), (), s32[]{:S(2)}) async-start(), calls=%async_computation.21 | async-start | bytes 4194304 | tf_op jit(solution)/shard_map/psum | solution.py:12
  941.4 3.4 copy-start.2
  944.4 186.4 %reduce-scatter.15.cloned.1.call-start = ((), (), s32[]{:S(2)}) async-start(), calls=%async_computation.19 | async-start | bytes 2228224 | tf_op jit(solution)/shard_map/reduce_scatter | solution.py:81
  947.0 2.3 copy-start.23
  949.4 3.6 copy-start.32
  955.2 3.9 copy-start.4
  955.2 3.9 copy-start.21
  959.1 2.0 copy-start.30
  963.3 1.7 copy-start.8
  969.4 237.3 %reduce-scatter.17.cloned.1.call-start = ((), (), s32[]{:S(2)}) async-start(), calls=%async_computation.20 | async-start | bytes 1179648 | tf_op jit(solution)/shard_map/reduce_scatter | solution.py:79
  1070.8 2.0 copy-start.19
  1072.9 3.7 copy-start.28
  1076.6 2.2 copy-start.17
  1078.9 2.2 copy-start.25
  1083.4 123.3 %copy-start.11 = (f32[1,64,512]{2,1,0:T(8,128)S(1)}, f32[1,64,512]{2,1,0:T(8,128)}, u32[]{:S(2)}) copy-start(f32[1,64,512]{2,1,0:T(8,128)} %multiply_add_fusion.1) | copy-start | bytes 393220
  1083.4 190.5 %copy-start.13 = (f32[1,64,512]{2,1,0:T(8,128)S(1)}, f32[1,64,512]{2,1,0:T(8,128)}, u32[]{:S(2)}) copy-start(f32[1,64,512]{2,1,0:T(8,128)} %copy-done.12) | copy-start | bytes 393220
  1083.4 190.5 %copy-start.15 = (f32[512]{0:T(512)S(1)}, f32[512]{0:T(512)}, u32[]{:S(2)}) copy-start(f32[512]{0:T(512)} %copy-done.14) | copy-start | bytes 6148
Sparse Core Ops, SparseCore 0:
  10.3 49.5 all-gather.3
  63.0 122.9 all-reduce.11
  188.4 60.8 reduce-scatter.6
  252.8 72.3 reduce-scatter.8
  456.8 43.4 all-gather.5
  503.4 122.9 all-reduce.9
  628.9 60.8 reduce-scatter.10
  693.9 72.3 reduce-scatter.12
  897.9 43.4 all-gather.7
  944.5 122.9 all-reduce.7
  1069.9 60.8 reduce-scatter.14
  1134.3 72.3 reduce-scatter.16
where the time goes:
time: 1290 us; the launch traced here: 1280 us
  waiting for transfers between devices  714 us (55%)
  blocking collectives  407 us (32%)
  matrix products  62.8 us (5%)
  local copies, waits for them, and re-layouts  59.1 us (5%)
  other arithmetic  23.3 us (2%)
  between operations  15.1 us (1%)
    psum x3, waiting for transfers between devices, broadcast(): return lax.psum(kept, axis)  295 us
    psum x3, blocking collectives, squares(): return lax.psum(jnp.sum(residual * residual, axis=(0, 1)), ('row', 'col'))  191 us
    reduce_scatter x3, waiting for transfers between devices, operate(): lax.psum_scatter(backward[None], 'row', scatter_dimension=1, tiled=True)  142 us
    reduce_scatter x3, waiting for transfers between devices, operate(): summed = lax.psum_scatter(spread, 'col', scatter_dimension=2, tiled=True)  139 us
    all_gather x3, waiting for transfers between devices, operate(): whole = lax.all_gather(piece, 'row', axis=1, tiled=True)  137 us
    psum x2, blocking collectives, shards(): curve = lax.psum(jnp.sum(direction * image, axis=(0, 1)), ('row', 'col'))  133 us
    all_to_all x3, blocking collectives, operate(): lax.all_to_all(lax.all_to_all(ordered, 'row', split_axis=0, concat_axis=0...  42.7 us
    all_to_all x3, blocking collectives, operate(): lax.all_to_all(ordered, 'row', split_axis=0, concat_axis=0, tiled=True)  39.9 us
  transfers between devices with their start and end apart: 12, of which 12 were waited for; matrix products, arithmetic and copies ran while one was open for 10% of the time, Pallas kernels for 0%

commit v1 on v0

--- a/solution.py
+++ b/solution.py
@@ -68,7 +68,9 @@
     share = piece.shape[1]
     width = piece.shape[2]
     sliver = share // cols_count
-    whole = lax.all_gather(piece, "row", axis=1, tiled=True)
+    whole = jnp.concatenate(
+        lax.all_to_all(jnp.stack([piece] * lax.axis_size("row")), "row", 0, 0), axis=1
+    )
     received = []
     for member in range(members):
         received.append(broadcast(whole[0], "col", my_row * members + member))

time: 1290 us -> 1210 us (0.938)
  waiting for transfers between devices: 714 us -> 584 us
  blocking collectives: 407 us -> 447 us
    all_gather x3 -> x0, waiting for transfers between devices: 137 us -> none  [operate(): whole = lax.all_gather(piece, 'row', axis=1, tiled=True)]
    all_to_all x0 -> x2, blocking collectives: none -> 40.4 us  [operate(): lax.all_to_all(jnp.stack([piece] * lax.axis_size('row')), 'row', 0, 0)]
    all_to_all x0 -> x1, waiting for transfers between devices: none -> 16 us  [operate(): lax.all_to_all(jnp.stack([piece] * lax.axis_size('row')), 'row', 0, 0)]
  transfers between devices with their start and end apart: 12 -> 10, of which waited for: 12 -> 10; matrix products, arithmetic and copies ran while one was open for 10% -> 11% of each run, Pallas kernels for 0% -> 0%
where the time goes in v1:
time: 1210 us; the launch traced here: 1200 us
  waiting for transfers between devices  584 us (48%)
  blocking collectives  447 us (37%)
  matrix products  62.9 us (5%)
  local copies, waits for them, and re-layouts  61.2 us (5%)
  other arithmetic  18.1 us (1%)
  between operations  15 us (1%)
    psum x3, waiting for transfers between devices, broadcast(): return lax.psum(kept, axis)  287 us
    psum x3, blocking collectives, squares(): return lax.psum(jnp.sum(residual * residual, axis=(0, 1)), ('row', 'col'))  191 us
    reduce_scatter x3, waiting for transfers between devices, operate(): lax.psum_scatter(backward[None], 'row', scatter_dimension=1, tiled=True)  143 us
    reduce_scatter x3, waiting for transfers between devices, operate(): summed = lax.psum_scatter(spread, 'col', scatter_dimension=2, tiled=True)  138 us
    psum x2, blocking collectives, shards(): curve = lax.psum(jnp.sum(direction * image, axis=(0, 1)), ('row', 'col'))  133 us
    all_to_all x3, blocking collectives, operate(): lax.all_to_all(lax.all_to_all(ordered, 'row', split_axis=0, concat_axis=0...  42.7 us
    all_to_all x2, blocking collectives, operate(): lax.all_to_all(jnp.stack([piece] * lax.axis_size('row')), 'row', 0, 0)  40.4 us
    all_to_all x3, blocking collectives, operate(): lax.all_to_all(ordered, 'row', split_axis=0, concat_axis=0, tiled=True)  39.9 us
  transfers between devices with their start and end apart: 10, of which 10 were waited for; matrix products, arithmetic and copies ran while one was open for 11% of the time, Pallas kernels for 0%

profile of v1, /device:TPU:1, one launch (start us, length us, event | category | flops | bytes accessed | tf_op | source)
XLA Modules:
  0.0 1197.8 jit_solution(15670423133662718970)
XLA Ops:
  7.2 2.0 stack.24
  9.2 7.5 all-to-all-start
  18.0 16.0 %all-to-all-done = f32[8,1,64,512]{3,2,1,0:T(8,128)S(1)} async-done(((f32[8,1,64,512]{3,2,1,0:T(8,128)}), f32[8,1,64,512]{3,2,1,0:T(8,128)S(1)}, u32[]{:S(2)}, u32[]{:S(2)}) %all-to-all-start) | async-done | bytes 1048608 | tf_op jit(solution)/shard_map/all_to_all | solution.py:72
  36.6 2.1 gather_fusion.1
  38.6 3.6 fusion.44
  42.2 2.2 fusion.20
  46.1 2.0 gather_fusion
  48.1 3.6 fusion.46
  51.7 2.2 fusion.22
  57.3 2.6 copy.49
  60.4 97.0 %all-reduce.12.cloned.1.call-done = (f32[4,128,512]{2,1,0:T(8,128)}, f32[4,128,512]{2,1,0:T(8,128)}) async-done(((f32[4,128,512]{2,1,0:T(8,128)}, f32[4,128,512]{2,1,0:T(8,128)}), (f32[4,128,512]{2,1,0:T(8,128)}, f32[4,128,512]{2,1,0:T(8,128)})) %all-reduce.12.cloned.1.call-update) | async-done | bytes 2097168 | tf_op jit(solution)/shard_map/psum | solution.py:12
  157.4 3.2 gather_fusion.3
  162.5 3.7 fusion.40
  166.2 2.2 fusion.16
  168.4 2.2 fusion.42
  170.6 2.3 fusion.48
  174.3 46.3 %reduce-scatter.7.cloned.1.call-done = f32[2,8,1,4,512]{4,1,3,0,2:T(8,128)} async-done(((f32[2,8,16,4,512]{4,1,3,0,2:T(8,128)}), f32[2,8,1,4,512]{4,1,3,0,2:T(8,128)}) %reduce-scatter.7.cloned.1.call-update) | async-done | bytes 131088 | tf_op jit(solution)/shard_map/reduce_scatter | solution.py:83
  221.6 13.3 %all_to_all.66 = f32[16,4,512]{2,1,0:T(4,128)S(1)} all-to-all(f32[16,4,512]{2,1,0:T(4,128)S(1)} %bitcast.103), channel_id=1, replica_groups=mesh['row'=8,'col'=16] {'row'}, dimensions={0} | all-to-all | bytes 262144 | tf_op jit(solution)/shard_map/all_to_all | solution.py:87
  234.9 14.2 %all_to_all.67 = f32[16,4,512]{2,1,0:T(4,128)S(1)} all-to-all(f32[16,4,512]{2,1,0:T(4,128)S(1)} %all_to_all.66), channel_id=1, replica_groups=mesh['row'=8,'col'=16] {'col'}, dimensions={0} | all-to-all | bytes 262144 | tf_op jit(solution)/shard_map/all_to_all | solution.py:86
  249.2 47.5 %reduce-scatter.9.cloned.1.call-done = f32[1,64,512]{2,1,0:T(8,128)} async-done(((f32[1,512,512]{2,1,0:T(8,128)}), f32[1,64,512]{2,1,0:T(8,128)}) %reduce-scatter.9.cloned.1.call-update) | async-done | bytes 131088 | tf_op jit(solution)/shard_map/reduce_scatter | solution.py:81
  297.6 66.3 %all-reduce = (f32[512]{0:T(512)S(1)}, f32[512]{0:T(512)S(1)}) all-reduce(f32[512]{0:T(512)S(1)} %get-tuple-element.4, f32[512]{0:T(512)S(1)} %get-tuple-element.3), channel_id=1, replica_groups=mesh['row'=8,'col'=16] {'row','col'}, use_global_device_ids=true, to_apply=%region_1.0 | all-reduce | flops 1024 | bytes 8192 | tf_op jit(solution)/shard_map/psum | solution.py:97
  364.9 62.5 %psum.88 = f32[512]{0:T(512)S(1)} all-reduce(f32[512]{0:T(512)S(1)} %get-tuple-element.15), channel_id=1, replica_groups=mesh['row'=8,'col'=16] {'row','col'}, use_global_device_ids=true, to_apply=%region_9.11 | all-reduce | flops 512 | bytes 4096 | tf_op jit(solution)/shard_map/psum | solution.py:97
  427.6 20.2 %all_to_all.68 = f32[8,1,64,512]{3,2,1,0:T(8,128)S(1)} all-to-all(f32[8,1,64,512]{3,2,1,0:T(8,128)S(1)} %stack.28), channel_id=1, replica_groups=mesh['row'=8,'col'=16] {'row'}, dimensions={0} | all-to-all | bytes 2097152 | tf_op jit(solution)/shard_map/all_to_all | solution.py:72
  449.7 2.1 gather_fusion.5
  451.8 2.1 gather_fusion.4
  453.9 3.6 fusion.36
  457.5 2.2 fusion.12
  461.1 2.5 stack.60
  463.6 2.0 fusion.38
  465.6 2.2 fusion.14
  471.3 2.6 copy.60
  474.4 95.2 %all-reduce.10.cloned.1.call-done = (f32[4,128,512]{2,1,0:T(8,128)}, f32[4,128,512]{2,1,0:T(8,128)}) async-done(((f32[4,128,512]{2,1,0:T(8,128)}, f32[4,128,512]{2,1,0:T(8,128)}), (f32[4,128,512]{2,1,0:T(8,128)}, f32[4,128,512]{2,1,0:T(8,128)})) %all-reduce.10.cloned.1.call-update) | async-done | bytes 2097168 | tf_op jit(solution)/shard_map/psum | solution.py:12
  569.6 3.2 gather_fusion.7
  574.8 3.7 fusion.32
  578.5 2.2 fusion.8
  580.7 2.1 fusion.34
  582.9 2.3 fusion.51
  586.7 46.2 %reduce-scatter.11.cloned.1.call-done = f32[2,8,1,4,512]{4,1,3,0,2:T(8,128)} async-done(((f32[2,8,16,4,512]{4,1,3,0,2:T(8,128)}), f32[2,8,1,4,512]{4,1,3,0,2:T(8,128)}) %reduce-scatter.11.cloned.1.call-update) | async-done | bytes 131088 | tf_op jit(solution)/shard_map/reduce_scatter | solution.py:83
  633.8 13.3 %all_to_all.69 = f32[16,4,512]{2,1,0:T(4,128)S(1)} all-to-all(f32[16,4,512]{2,1,0:T(4,128)S(1)} %bitcast.104), channel_id=1, replica_groups=mesh['row'=8,'col'=16] {'row'}, dimensions={0} | all-to-all | bytes 262144 | tf_op jit(solution)/shard_map/all_to_all | solution.py:87
  647.1 14.3 %all_to_all.70 = f32[16,4,512]{2,1,0:T(4,128)S(1)} all-to-all(f32[16,4,512]{2,1,0:T(4,128)S(1)} %all_to_all.69), channel_id=1, replica_groups=mesh['row'=8,'col'=16] {'col'}, dimensions={0} | all-to-all | bytes 262144 | tf_op jit(solution)/shard_map/all_to_all | solution.py:86
  661.5 47.7 %reduce-scatter.13.cloned.1.call-done = f32[1,64,512]{2,1,0:T(8,128)} async-done(((f32[1,512,512]{2,1,0:T(8,128)}), f32[1,64,512]{2,1,0:T(8,128)}) %reduce-scatter.13.cloned.1.call-update) | async-done | bytes 131088 | tf_op jit(solution)/shard_map/reduce_scatter | solution.py:81
  710.1 66.3 %psum.91 = f32[512]{0:T(512)S(1)} all-reduce(f32[512]{0:T(512)S(1)} %multiply_reduce_fusion.2), channel_id=1, replica_groups=mesh['row'=8,'col'=16] {'row','col'}, use_global_device_ids=true, to_apply=%region_15.17 | all-reduce | flops 512 | bytes 4096 | tf_op jit(solution)/shard_map/psum | solution.py:107
  777.4 62.5 %psum.92 = f32[512]{0:T(512)S(1)} all-reduce(f32[512]{0:T(512)S(1)} %get-tuple-element.13), channel_id=1, replica_groups=mesh['row'=8,'col'=16] {'row','col'}, use_global_device_ids=true, to_apply=%region_17.19 | all-reduce | flops 512 | bytes 4096 | tf_op jit(solution)/shard_map/psum | solution.py:97
  840.7 20.2 %all_to_all.71 = f32[8,1,64,512]{3,2,1,0:T(8,128)S(1)} all-to-all(f32[8,1,64,512]{3,2,1,0:T(8,128)S(1)} %stack.62), channel_id=1, replica_groups=mesh['row'=8,'col'=16] {'row'}, dimensions={0} | all-to-all | bytes 2097152 | tf_op jit(solution)/shard_map/all_to_all | solution.py:72
  862.7 2.2 gather_fusion.9
  864.9 2.3 gather_fusion.8
  867.3 3.7 fusion.28
  870.9 2.2 fusion.4
  874.6 2.5 stack.64
  877.1 2.0 fusion.30
  879.1 2.2 fusion.6
  884.8 2.6 copy.71
  887.7 95.0 %all-reduce.8.cloned.1.call-done = (f32[4,128,512]{2,1,0:T(8,128)}, f32[4,128,512]{2,1,0:T(8,128)}) async-done(((f32[4,128,512]{2,1,0:T(8,128)}, f32[4,128,512]{2,1,0:T(8,128)}), (f32[4,128,512]{2,1,0:T(8,128)}, f32[4,128,512]{2,1,0:T(8,128)})) %all-reduce.8.cloned.1.call-update) | async-done | bytes 2097168 | tf_op jit(solution)/shard_map/psum | solution.py:12
  982.6 3.4 gather_fusion.11
  986.0 2.0 gather_fusion.10
  988.1 3.7 fusion.24
  991.8 2.2 fusion
  994.0 2.2 fusion.26
  996.2 2.3 fusion.54
  999.9 46.0 %reduce-scatter.15.cloned.1.call-done = f32[2,8,1,4,512]{4,1,3,0,2:T(8,128)} async-done(((f32[2,8,16,4,512]{4,1,3,0,2:T(8,128)}), f32[2,8,1,4,512]{4,1,3,0,2:T(8,128)}) %reduce-scatter.15.cloned.1.call-update) | async-done | bytes 131088 | tf_op jit(solution)/shard_map/reduce_scatter | solution.py:83
  1046.9 13.3 %all_to_all.72 = f32[16,4,512]{2,1,0:T(4,128)S(1)} all-to-all(f32[16,4,512]{2,1,0:T(4,128)S(1)} %bitcast.105), channel_id=1, replica_groups=mesh['row'=8,'col'=16] {'row'}, dimensions={0} | all-to-all | bytes 262144 | tf_op jit(solution)/shard_map/all_to_all | solution.py:87
  1060.2 14.2 %all_to_all.73 = f32[16,4,512]{2,1,0:T(4,128)S(1)} all-to-all(f32[16,4,512]{2,1,0:T(4,128)S(1)} %all_to_all.72), channel_id=1, replica_groups=mesh['row'=8,'col'=16] {'col'}, dimensions={0} | all-to-all | bytes 262144 | tf_op jit(solution)/shard_map/all_to_all | solution.py:86
  1074.4 47.5 %reduce-scatter.17.cloned.1.call-done = f32[1,64,512]{2,1,0:T(8,128)} async-done(((f32[1,512,512]{2,1,0:T(8,128)}), f32[1,64,512]{2,1,0:T(8,128)}) %reduce-scatter.17.cloned.1.call-update) | async-done | bytes 131088 | tf_op jit(solution)/shard_map/reduce_scatter | solution.py:81
  1122.9 66.3 %psum.95 = f32[512]{0:T(512)S(1)} all-reduce(f32[512]{0:T(512)S(1)} %multiply_reduce_fusion), channel_id=1, replica_groups=mesh['row'=8,'col'=16] {'row','col'}, use_global_device_ids=true, to_apply=%region_23.25 | all-reduce | flops 512 | bytes 4096 | tf_op jit(solution)/shard_map/psum | solution.py:107
  (141 shorter events, 41.8 us)
Async XLA Ops:
  7.2 9.6 copy-start.36
  9.2 24.8 %all-to-all-start = ((f32[8,1,64,512]{3,2,1,0:T(8,128)}), f32[8,1,64,512]{3,2,1,0:T(8,128)S(1)}, u32[]{:S(2)}, u32[]{:S(2)}) async-start(f32[8,1,64,512]{3,2,1,0:T(8,128)} %stack.24), calls=%async_computation | async-start | bytes 2097152 | tf_op jit(solution)/shard_map/all_to_all | solution.py:72
  16.7 140.7 %all-reduce.12.cloned.1.call-start = ((), (), s32[]{:S(2)}) async-start(), calls=%async_computation.23 | async-start | bytes 4194304 | tf_op jit(solution)/shard_map/psum | solution.py:12
  18.0 18.4 %copy-start.25 = (s32[2,1,8,2]{2,3,1,0:T(2,128)S(1)}, s32[2,1,8,2]{2,3,1,0:T(2,128)}, u32[]{:S(2)}) copy-start(s32[2,1,8,2]{2,3,1,0:T(2,128)} %param.8) | copy-start | bytes 388
  35.7 184.9 %reduce-scatter.7.cloned.1.call-start = ((), (), s32[]{:S(2)}) async-start(), calls=%async_computation.15 | async-start | bytes 2228224 | tf_op jit(solution)/shard_map/reduce_scatter | solution.py:83
  36.4 417.4 %copy-start.21 = (pred[8]{0:T(512)(128)(4,1)}, pred[8]{0:T(512)(128)(4,1)S(1)}, u32[]{:S(2)}) copy-start(pred[8]{0:T(512)(128)(4,1)S(1)} %get-tuple-element.37) | copy-start | bytes 28
  36.4 427.2 %copy-start.19 = (pred[8]{0:T(512)(128)(4,1)}, pred[8]{0:T(512)(128)(4,1)S(1)}, u32[]{:S(2)}) copy-start(pred[8]{0:T(512)(128)(4,1)S(1)} %get-tuple-element.41) | copy-start | bytes 28
  36.4 538.3 %copy-start.17 = (pred[8]{0:T(512)(128)(4,1)}, pred[8]{0:T(512)(128)(4,1)S(1)}, u32[]{:S(2)}) copy-start(pred[8]{0:T(512)(128)(4,1)S(1)} %get-tuple-element.39) | copy-start | bytes 28
  36.5 544.3 %copy-start.15 = (pred[8]{0:T(512)(128)(4,1)}, pred[8]{0:T(512)(128)(4,1)S(1)}, u32[]{:S(2)}) copy-start(pred[8]{0:T(512)(128)(4,1)S(1)} %get-tuple-element.17) | copy-start | bytes 28
  36.5 413.2 %copy-start.35 = (s32[1024]{0:T(1024)}, s32[1024]{0:T(1024)S(1)}, u32[]{:S(2)}) copy-start(s32[1024]{0:T(1024)S(1)} %get-tuple-element.47) | copy-start | bytes 12292
  36.5 415.3 %copy-start.34 = (s32[1024]{0:T(1024)}, s32[1024]{0:T(1024)S(1)}, u32[]{:S(2)}) copy-start(s32[1024]{0:T(1024)S(1)} %get-tuple-element.48) | copy-start | bytes 12292
  36.5 421.0 %copy-start.30 = (s32[8]{0:T(128)}, s32[8]{0:T(128)S(1)}, u32[]{:S(2)}) copy-start(s32[8]{0:T(128)S(1)} %get-tuple-element.36) | copy-start | bytes 100
  36.5 429.1 %copy-start.28 = (s32[8]{0:T(128)}, s32[8]{0:T(128)S(1)}, u32[]{:S(2)}) copy-start(s32[8]{0:T(128)S(1)} %get-tuple-element.34) | copy-start | bytes 100
  36.5 542.0 %copy-start.26 = (s32[8]{0:T(128)}, s32[8]{0:T(128)S(1)}, u32[]{:S(2)}) copy-start(s32[8]{0:T(128)S(1)} %get-tuple-element.35) | copy-start | bytes 100
  36.5 546.4 %copy-start.23 = (s32[8]{0:T(128)}, s32[8]{0:T(128)S(1)}, u32[]{:S(2)}) copy-start(s32[8]{0:T(128)S(1)} %get-tuple-element.33) | copy-start | bytes 100
  36.6 2.1 copy-start
  53.9 1.7 copy-start.3
  60.0 236.7 %reduce-scatter.9.cloned.1.call-start = ((), (), s32[]{:S(2)}) async-start(), calls=%async_computation.16 | async-start | bytes 1179648 | tf_op jit(solution)/shard_map/reduce_scatter | solution.py:81
  60.4 509.2 %copy-start.33 = (s32[1024]{0:T(1024)}, s32[1024]{0:T(1024)S(1)}, u32[]{:S(2)}) copy-start(s32[1024]{0:T(1024)S(1)} %get-tuple-element.45) | copy-start | bytes 12292
  60.4 512.5 %copy-start.32 = (s32[1024]{0:T(1024)}, s32[1024]{0:T(1024)S(1)}, u32[]{:S(2)}) copy-start(s32[1024]{0:T(1024)S(1)} %get-tuple-element.46) | copy-start | bytes 12292
  172.9 123.7 %copy-start.6 = (f32[1,64,512]{2,1,0:T(8,128)S(1)}, f32[1,64,512]{2,1,0:T(8,128)}, u32[]{:S(2)}) copy-start(f32[1,64,512]{2,1,0:T(8,128)} %param.6) | copy-start | bytes 393220
  174.3 395.3 %all-reduce.10.cloned.1.call-start = ((), (), s32[]{:S(2)}) async-start(), calls=%async_computation.22 | async-start | bytes 4194304 | tf_op jit(solution)/shard_map/psum | solution.py:12
  363.9 83.9 %copy-start.9 = (f32[512]{0:T(512)}, f32[512]{0:T(512)S(1)}, u32[]{:S(2)}) copy-start(f32[512]{0:T(512)S(1)} %div.15) | copy-start | bytes 6148
  364.9 62.6 %copy-start.7 = (f32[1,64,512]{2,1,0:T(8,128)}, f32[1,64,512]{2,1,0:T(8,128)S(1)}, u32[]{:S(2)}) copy-start(f32[1,64,512]{2,1,0:T(8,128)S(1)} %get-tuple-element.16) | copy-start | bytes 393220
  449.5 183.3 %reduce-scatter.11.cloned.1.call-start = ((), (), s32[]{:S(2)}) async-start(), calls=%async_computation.17 | async-start | bytes 2228224 | tf_op jit(solution)/shard_map/reduce_scatter | solution.py:83
  459.7 3.9 copy-start.2
  467.8 1.7 copy-start.5
  473.9 235.3 %reduce-scatter.13.cloned.1.call-start = ((), (), s32[]{:S(2)}) async-start(), calls=%async_computation.18 | async-start | bytes 1179648 | tf_op jit(solution)/shard_map/reduce_scatter | solution.py:81
  585.2 191.2 %copy-start.8 = (f32[1,64,512]{2,1,0:T(8,128)S(1)}, f32[1,64,512]{2,1,0:T(8,128)}, u32[]{:S(2)}) copy-start(f32[1,64,512]{2,1,0:T(8,128)} %copy-done.7) | copy-start | bytes 393220
  586.6 396.0 %all-reduce.8.cloned.1.call-start = ((), (), s32[]{:S(2)}) async-start(), calls=%async_computation.21 | async-start | bytes 4194304 | tf_op jit(solution)/shard_map/psum | solution.py:12
  776.4 1.0 copy-start.11
  840.0 0.6 copy-start.13
  862.5 183.4 %reduce-scatter.15.cloned.1.call-start = ((), (), s32[]{:S(2)}) async-start(), calls=%async_computation.19 | async-start | bytes 2228224 | tf_op jit(solution)/shard_map/reduce_scatter | solution.py:83
  864.9 2.3 copy-start.22
  867.3 3.7 copy-start.31
  873.2 3.9 copy-start.1
  873.2 3.9 copy-start.20
  877.1 2.0 copy-start.29
  881.3 1.7 copy-start.4
  887.4 234.6 %reduce-scatter.17.cloned.1.call-start = ((), (), s32[]{:S(2)}) async-start(), calls=%async_computation.20 | async-start | bytes 1179648 | tf_op jit(solution)/shard_map/reduce_scatter | solution.py:81
  986.0 2.0 copy-start.18
  988.0 3.7 copy-start.27
  991.8 2.2 copy-start.16
  994.0 2.2 copy-start.24
  998.5 190.7 %copy-start.14 = (f32[512]{0:T(512)S(1)}, f32[512]{0:T(512)}, u32[]{:S(2)}) copy-start(f32[512]{0:T(512)} %copy-done.13) | copy-start | bytes 6148
  998.5 190.7 %copy-start.10 = (f32[512]{0:T(512)S(1)}, f32[512]{0:T(512)}, u32[]{:S(2)}) copy-start(f32[512]{0:T(512)} %copy-done.9) | copy-start | bytes 6148
  998.6 190.7 %copy-start.12 = (f32[512]{0:T(512)S(1)}, f32[512]{0:T(512)}, u32[]{:S(2)}) copy-start(f32[512]{0:T(512)} %copy-done.11) | copy-start | bytes 6148
Sparse Core Ops, SparseCore 0:
  35.8 121.4 all-reduce.11
  159.7 60.8 reduce-scatter.6
  224.3 72.3 reduce-scatter.8
  449.6 119.9 all-reduce.9
  572.0 60.8 reduce-scatter.10
  636.8 72.3 reduce-scatter.12
  862.6 119.9 all-reduce.7
  985.0 60.8 reduce-scatter.14
  1049.5 72.3 reduce-scatter.16
